TPU v7x, 32 devices: a whole 2x2x4 slice. The times are simulated.
32 devices in a mesh: groups: 2 (over y), obs: 4 (over z), hid: 2 (over x), rep: 2 (over core).
Axes of the slice: x: 2, y: 2, z: 4, core: 2. Of those that a mesh axis runs over, the one named last changes fastest.
Arguments:
- particles: float32 [8, 128, 512], P(('groups', 'obs')), parts along dimension 0, may hold values from -6 to 6
- obs_embed: bfloat16 [32768, 256], P(('groups', 'obs', 'rep')), parts along dimension 0, may hold values from -6 to 6
- step_index: int32 [2], P('groups'), parts along dimension 0, may hold values from 1 to 63
- noise: float32 [8, 128, 512], P('groups', 'obs'), parts along dimension 0, may hold values from -6 to 6
- w_query: bfloat16 [512, 2048], P(None, 'hid'), may hold values from -0.25 to 0.25
- w_key: bfloat16 [256, 2048], P(None, 'hid'), may hold values from -0.375 to 0.375
- w_value: bfloat16 [256, 2048], P(None, 'hid'), may hold values from -0.375 to 0.375
- w_time: bfloat16 [256, 16], P(None, 'hid'), may hold values from -0.375 to 0.375
- w_score: bfloat16 [2048, 512], P('hid'), may hold values from -0.0009765625 to 0.0009765625
- prior_in: bfloat16 [512, 2048], P(None, 'hid'), may hold values from -0.25 to 0.25
- prior_time: bfloat16 [256, 2048], P(None, 'hid'), may hold values from -0.375 to 0.375
- prior_out: bfloat16 [2048, 512], P('hid'), may hold values from -7.6293945e-06 to 7.6293945e-06
Outputs:
- updated: float32 [8, 128, 512], P('groups', 'obs'), parts along dimension 0
- score_total: float32 [8, 128, 512], P('groups', 'obs'), parts along dimension 0
There are 2 independent parts, one for each index of `groups`. A program takes and returns all parts, laid end to end along the dimension named above; an argument that names none is the same for every part. Nothing has to cross between parts.
All inputs are finite; a program needn't handle non-finite values.
Results may differ from a plain program's by a relative error of at most 0.0042.
Values may be sent and summed in bfloat16 or wider, within the bound.
No kernel may reach another device: no remote copies, remote signals or barrier semaphores. Data moves between devices by JAX's collectives and lax.ppermute only.
A program may use at most 64 MiB of HBM per device.

v0:
```python
import math
import jax
import jax.numpy as jnp
from jax import lax
from jax.sharding import PartitionSpec as P

DH = 128
STEPS = 64
SIG_LO = 0.05
SIG_HI = 1.0


def passed_along(shard, axis, by):
    size = lax.axis_size(axis)
    return lax.ppermute(shard, axis, [(i, (i + by) % size) for i in range(size)])


def plan(step_index, feature_count):
    level = step_index[0].astype(jnp.float32)
    growth = math.log(SIG_HI / SIG_LO) / (STEPS - 1)
    sigma_now = SIG_LO * jnp.exp(growth * level)
    sigma_prev = SIG_LO * jnp.exp(growth * (level - 1.0))
    delta = sigma_now * sigma_now - sigma_prev * sigma_prev
    halves = feature_count // 2
    frequency = jnp.exp(-math.log(1000.0) / halves * jnp.arange(halves).astype(jnp.float32))
    angles = 10.0 * jnp.log(sigma_now) * frequency
    features = jnp.concatenate([jnp.sin(angles), jnp.cos(angles)])[None, :].astype(jnp.bfloat16)
    return (features, delta)


def pair_pool(queries, keys, values, head_bias):
    count = queries.shape[0]
    query_heads = queries.reshape(count, -1, DH)
    key_heads = keys.reshape(keys.shape[0], -1, DH)
    value_heads = values.reshape(values.shape[0], -1, DH)
    scores = jnp.einsum("phd,jhd->phj", query_heads, key_heads, preferred_element_type=jnp.float32)
    weights = jax.nn.silu(scores * (1.0 / math.sqrt(DH)) + head_bias[None, :, None]).astype(
        jnp.bfloat16
    )
    pooled = jnp.einsum("phj,jhd->phd", weights, value_heads, preferred_element_type=jnp.float32)
    return pooled.reshape(count, -1)


def on_device(
    particles,
    obs_embed,
    step_index,
    noise,
    w_query,
    w_key,
    w_value,
    w_time,
    w_score,
    prior_in,
    prior_time,
    prior_out,
):
    obs_count = lax.axis_size("obs")
    rep_count = lax.axis_size("rep")
    features, delta = plan(step_index, w_time.shape[0])
    head_bias = jnp.dot(features, w_time, preferred_element_type=jnp.float32)[0]
    keys = jnp.dot(obs_embed, w_key, preferred_element_type=jnp.float32).astype(jnp.bfloat16)
    values = jnp.dot(obs_embed, w_value, preferred_element_type=jnp.float32).astype(jnp.bfloat16)
    home = particles[0]
    block_rows = home.shape[0]
    width = home.shape[1]
    stripe = block_rows // obs_count
    owned = home.reshape(obs_count, stripe, width)
    theta_owner = lax.all_to_all(owned, "obs", split_axis=0, concat_axis=0, tiled=True)
    moving = home.astype(jnp.bfloat16)

    def pool(travel):
        queries = jnp.dot(travel, w_query, preferred_element_type=jnp.float32).astype(jnp.bfloat16)
        return pair_pool(queries, keys, values, head_bias)

    score_weight = w_score.astype(jnp.float32)

    def turn(turn_index, cycle_state):
        arrived = passed_along(cycle_state[0], "obs", 1)
        totals = passed_along(cycle_state[1], "obs", 1)
        return (arrived, totals + pool(arrived))

    cycle_state = lax.fori_loop(0, obs_count - 1, turn, (moving, pool(moving)))
    pieces = cycle_state[1].reshape(obs_count, stripe, -1)
    flat = pieces.reshape(-1, pieces.shape[-1])
    result = jnp.dot(
        flat, score_weight, precision=lax.Precision.HIGHEST, preferred_element_type=jnp.float32
    )
    pieces = result.reshape(pieces.shape[:-1] + (width,))
    received = lax.all_to_all(pieces, "obs", split_axis=0, concat_axis=0, tiled=True)
    summed = jnp.roll(received, 1, axis=0)
    owner_rows = theta_owner.reshape(block_rows, width)
    share = block_rows // rep_count
    start = lax.axis_index("rep") * share
    my_rows = lax.dynamic_slice_in_dim(owner_rows, start, share, 0).astype(jnp.bfloat16)
    prior_pre = jnp.dot(my_rows, prior_in, preferred_element_type=jnp.float32) + jnp.dot(
        features, prior_time, preferred_element_type=jnp.float32
    )
    prior_hidden = jax.nn.silu(prior_pre).astype(jnp.bfloat16)
    prior_part = jnp.dot(prior_hidden, prior_out, preferred_element_type=jnp.float32)
    total_count = obs_embed.shape[0] * obs_count * rep_count
    scores_flat = summed.reshape(block_rows, width)
    current = lax.dynamic_slice_in_dim(scores_flat, start, share, 0)
    scores_flat = lax.dynamic_update_slice_in_dim(
        scores_flat, current - (total_count - 1) * prior_part, start, 0
    )
    score_total = lax.psum(scores_flat, ("hid", "rep")).reshape(obs_count, stripe, width)
    updated = theta_owner + delta * score_total + jnp.sqrt(delta) * noise
    return (updated, score_total)


def solution(mesh):
    in_specs = (
        P(("groups", "obs"), None, None),
        P(("groups", "obs", "rep"), None),
        P("groups"),
        P("groups", "obs", None),
        P(None, "hid"),
        P(None, "hid"),
        P(None, "hid"),
        P(None, "hid"),
        P("hid", None),
        P(None, "hid"),
        P(None, "hid"),
        P("hid", None),
    )
    out_specs = (P("groups", "obs", None), P("groups", "obs", None))
    return jax.shard_map(
        on_device, mesh=mesh, in_specs=in_specs, out_specs=out_specs, check_vma=False
    )
```

profile of v0, /device:TPU:0, one launch (start us, length us, event | category | flops | bytes accessed | tf_op | source)
XLA Modules:
  0.0 154.7 jit_solution(1549332694135412617)
XLA Ops:
  7.2 0.0 copy-start
  8.1 0.3 copy-done
  8.4 4.3 %convolution_convert_fusion.2 = bf16[2048,1024]{0,1:T(8,128)(2,1)} fusion(bf16[2048,256]{1,0:T(8,128)(2,1)S(1)} %copy-done, bf16[256,1024]{1,0:T(8,128)(2,1)} %param.20), kind=kOutput, calls=%fused_computation.23 | convolution fusion | flops 1075838976 | bytes 5767168 | tf_op jit(solution)/shard_map/dot_general | solution.py:63
  12.8 0.0 copy-done.4
  12.8 3.3 %convolution_convert_fusion.1 = bf16[2048,1024]{0,1:T(8,128)(2,1)} fusion(bf16[2048,256]{1,0:T(8,128)(2,1)S(1)} %copy-done, bf16[256,1024]{1,0:T(8,128)(2,1)S(1)} %copy-done.4), kind=kOutput, calls=%fused_computation.22 | convolution fusion | flops 1075838976 | bytes 5767168 | tf_op jit(solution)/shard_map/dot_general | solution.py:62
  16.0 0.0 copy-done.2
  16.1 0.0 copy-start.7
  16.1 0.0 copy-start.1
  16.1 6.5 %copy.19 = bf16[2048,1024]{1,0:T(8,128)(2,1)} copy(bf16[2048,1024]{0,1:T(8,128)(2,1)} %convolution_convert_fusion.1) | data formatting | bytes 8388608 | tf_op jit(solution)/shard_map/while | solution.py:83
  22.6 0.0 copy-done.7
  22.6 0.1 fusion.35
  22.7 0.3 fusion.21
  23.0 8.8 %fusion.20 = f32[8,128,128]{2,1,0:T(8,128)} fusion(bf16[2048,8,128]{0,2,1:T(8,128)(2,1)} %bitcast.116, bf16[2048,8,128]{0,2,1:T(8,128)(2,1)} %bitcast.115, f32[8]{0:T(128)S(1)} %bitcast.124, bf16[16,8,8,128]{3,2,1,0:T(8,128)(2,1)S(1)} %fusion.21), kind=kOutput, calls=%fused_computation.24 | convolution fusion | flops 1088421888 | bytes 9175072 | tf_op jit(solution)/shard_map/phj,jhd->phd/dot_general | solution.py:40
  31.9 56.9 %while.12 = (s32[]{:T(128)}, bf16[128,512]{1,0:T(8,128)(2,1)S(1)}, f32[128,1024]{0,1:T(8,128)}, bf16[512,1024]{1,0:T(8,128)(2,1)S(1)}, bf16[2048,1024]{1,0:T(8,1...) while((s32[]{:T(128)}, bf16[128,512]{1,0:T(8,128)(2,1)S(1)}, ...), condition=%wide.region_1.2_spmd, body=%wide.region_0.1_spmd.sunk | while | flops 1222901760 | bytes 15073477 | solution.py:83
  31.9 3.0 %collective-permute-start = (bf16[128,512]{1,0:T(8,128)(2,1)S(1)}, bf16[128,512]{1,0:T(8,128)(2,1)S(1)}, u32[]{:S(2)}, u32[]{:S(2)}) collective-permute-start(bf16[128,512]{1,0:T(8,128)(2,1)S(1)} %get-tuple-element.115), channel_id=1, source_target_pairs={{0,4},{4,8},{8,12},{12,0},{1,5},{5,9},{9,13},{13,1},{2,6},{6,10},{... | collective-permute-start | bytes 393224 | tf_op jit(solution)/shard_map/while/body/eval_jaxpr/ppermute | solution.py:15
  34.9 1.6 %collective-permute-start.1 = (f32[128,1024]{0,1:T(8,128)}, f32[128,1024]{0,1:T(8,128)S(1)}, u32[]{:S(2)}, u32[]{:S(2)}) collective-permute-start(f32[128,1024]{0,1:T(8,128)} %get-tuple-element.116), channel_id=1, source_target_pairs={{0,4},{4,8},{8,12},{12,0},{1,5},{5,9},{9,13},{13,1},{2,6},{6,10},{... | collective-permute-start | bytes 1572872 | tf_op jit(solution)/shard_map/while/body/eval_jaxpr/ppermute | solution.py:15
  36.5 4.8 %collective-permute-done = bf16[128,512]{1,0:T(8,128)(2,1)S(1)} collective-permute-done((bf16[128,512]{1,0:T(8,128)(2,1)S(1)}, bf16[128,512]{1,0:T(8,128)(2,1)S(1)}, u32[]{:S(2)}, u32[]{:S(2)}) %collective-permute-start) | collective-permute-done | bytes 131104 | tf_op jit(solution)/shard_map/while/body/eval_jaxpr/ppermute | solution.py:15
  41.2 0.3 fusion.72
  41.6 6.3 %fusion.73 = f32[8,128,128]{1,2,0:T(8,128)S(1)} fusion(bf16[2048,8,128]{0,2,1:T(8,128)(2,1)} %bitcast.117, f32[8]{0:T(128)S(1)} %bitcast.125, bf16[16,8,8,128]{3,2,1,0:T(8,128)(2,1)S(1)} %fusion.72, bf16[2048,1024]{1,0:T(8,128)(2,1)} %get-tuple-element.126), kind=kOutput, calls=%fused_computation.8.clone.1 | convolution fusion | flops 1088421888 | bytes 9175072 | tf_op jit(solution)/shard_map/while/body/eval_jaxpr/phj,jhd->phd/dot_general | solution.py:40
  47.9 3.8 %collective-permute-done.1 = f32[128,1024]{0,1:T(8,128)S(1)} collective-permute-done((f32[128,1024]{0,1:T(8,128)}, f32[128,1024]{0,1:T(8,128)S(1)}, u32[]{:S(2)}, u32[]{:S(2)}) %collective-permute-start.1) | collective-permute-done | bytes 524320 | tf_op jit(solution)/shard_map/while/body/eval_jaxpr/ppermute | solution.py:15
  51.6 0.9 bitcast_add_fusion.2
  52.5 0.0 collective-permute-start
  52.5 1.3 collective-permute-start.1
  53.8 6.9 %collective-permute-done = bf16[128,512]{1,0:T(8,128)(2,1)S(1)} collective-permute-done((bf16[128,512]{1,0:T(8,128)(2,1)S(1)}, bf16[128,512]{1,0:T(8,128)(2,1)S(1)}, u32[]{:S(2)}, u32[]{:S(2)}) %collective-permute-start) | collective-permute-done | bytes 131104 | tf_op jit(solution)/shard_map/while/body/eval_jaxpr/ppermute | solution.py:15
  60.7 0.3 fusion.72
  61.1 6.3 %fusion.73 = f32[8,128,128]{1,2,0:T(8,128)S(1)} fusion(bf16[2048,8,128]{0,2,1:T(8,128)(2,1)} %bitcast.117, f32[8]{0:T(128)S(1)} %bitcast.125, bf16[16,8,8,128]{3,2,1,0:T(8,128)(2,1)S(1)} %fusion.72, bf16[2048,1024]{1,0:T(8,128)(2,1)} %get-tuple-element.126), kind=kOutput, calls=%fused_computation.8.clone.1 | convolution fusion | flops 1088421888 | bytes 9175072 | tf_op jit(solution)/shard_map/while/body/eval_jaxpr/phj,jhd->phd/dot_general | solution.py:40
  67.4 2.9 %collective-permute-done.1 = f32[128,1024]{0,1:T(8,128)S(1)} collective-permute-done((f32[128,1024]{0,1:T(8,128)}, f32[128,1024]{0,1:T(8,128)S(1)}, u32[]{:S(2)}, u32[]{:S(2)}) %collective-permute-start.1) | collective-permute-done | bytes 524320 | tf_op jit(solution)/shard_map/while/body/eval_jaxpr/ppermute | solution.py:15
  70.2 0.9 bitcast_add_fusion.2
  71.1 0.0 collective-permute-start
  71.1 0.0 collective-permute-start.1
  71.1 8.2 %collective-permute-done = bf16[128,512]{1,0:T(8,128)(2,1)S(1)} collective-permute-done((bf16[128,512]{1,0:T(8,128)(2,1)S(1)}, bf16[128,512]{1,0:T(8,128)(2,1)S(1)}, u32[]{:S(2)}, u32[]{:S(2)}) %collective-permute-start) | collective-permute-done | bytes 131104 | tf_op jit(solution)/shard_map/while/body/eval_jaxpr/ppermute | solution.py:15
  79.3 0.3 fusion.72
  79.7 6.3 %fusion.73 = f32[8,128,128]{1,2,0:T(8,128)S(1)} fusion(bf16[2048,8,128]{0,2,1:T(8,128)(2,1)} %bitcast.117, f32[8]{0:T(128)S(1)} %bitcast.125, bf16[16,8,8,128]{3,2,1,0:T(8,128)(2,1)S(1)} %fusion.72, bf16[2048,1024]{1,0:T(8,128)(2,1)} %get-tuple-element.126), kind=kOutput, calls=%fused_computation.8.clone.1 | convolution fusion | flops 1088421888 | bytes 9175072 | tf_op jit(solution)/shard_map/while/body/eval_jaxpr/phj,jhd->phd/dot_general | solution.py:40
  86.0 2.0 %collective-permute-done.1 = f32[128,1024]{0,1:T(8,128)S(1)} collective-permute-done((f32[128,1024]{0,1:T(8,128)}, f32[128,1024]{0,1:T(8,128)S(1)}, u32[]{:S(2)}, u32[]{:S(2)}) %collective-permute-start.1) | collective-permute-done | bytes 524320 | tf_op jit(solution)/shard_map/while/body/eval_jaxpr/ppermute | solution.py:15
  87.9 0.9 bitcast_add_fusion.2
  88.8 2.2 %fusion.36 = f32[128,512]{1,0:T(8,128)S(1)} fusion(f32[128,1024]{0,1:T(8,128)} %get-tuple-element.39, bf16[1024,512]{1,0:T(8,128)(2,1)} %param.22), kind=kOutput, calls=%fused_computation.49 | convolution fusion | flops 805306368 | bytes 1835008 | tf_op jit(solution)/shard_map/dot_general | solution.py:86
  91.0 9.5 %all_to_all.10 = f32[4,32,512]{2,1,0:T(8,128)S(1)} all-to-all(f32[4,32,512]{2,1,0:T(8,128)S(1)} %bitcast.119), channel_id=1, replica_groups=mesh['groups'=2,'obs'=4,'hid'=2,'rep'=2] {'obs'}, dimensions={0} | all-to-all | bytes 524288 | tf_op jit(solution)/shard_map/all_to_all | solution.py:90
  100.5 3.4 %all-to-all-start = ((f32[4,32,512]{2,1,0:T(8,128)}), f32[4,32,512]{2,1,0:T(8,128)S(1)}, u32[]{:S(2)}, u32[]{:S(2)}) async-start(f32[4,32,512]{2,1,0:T(8,128)} %bitcast.120), calls=%async_computation | async-start | bytes 524288 | tf_op jit(solution)/shard_map/all_to_all | solution.py:69
  103.9 0.0 all-reduce.2.cloned.1.call-start
  103.9 1.2 fusion.37
  105.2 5.4 %all-to-all-done = f32[4,32,512]{2,1,0:T(8,128)S(1)} async-done(((f32[4,32,512]{2,1,0:T(8,128)}), f32[4,32,512]{2,1,0:T(8,128)S(1)}, u32[]{:S(2)}, u32[]{:S(2)}) %all-to-all-start) | async-done | bytes 262176 | tf_op jit(solution)/shard_map/all_to_all | solution.py:69
  110.6 1.7 %fusion.23 = f32[128,512]{1,0:T(8,128)S(1)} fusion(f32[128,512]{1,0:T(8,128)S(1)} %bitcast.121, s32[]{:T(128)S(6)} %select_n.2, bf16[1024,512]{1,0:T(8,128)(2,1)S(1)} %copy-done.6, bf16[512,1024]{1,0:T(8,128)(2,1)} %param.23, f32[1024]{0:T(1024)S(1)} %bitcast.123, f32[128,512]{1,0:T(8,128)S(1)} %bitcast.118), kind=kOutput, calls=%fused_computation.30 | convolution fusion | flops 134676480 | bytes 2429952 | tf_op jit(solution)/shard_map/dot_general | solution.py:100
  112.4 0.0 copy-start.3
  112.4 0.7 copy-done.3
  113.1 0.0 all-reduce.2.cloned.1.call-update
  113.2 31.3 %all-reduce.2.cloned.1.call-done = f32[4,32,512]{2,1,0:T(8,128)} async-done(((f32[4,32,512]{2,1,0:T(8,128)}), f32[4,32,512]{2,1,0:T(8,128)}) %all-reduce.2.cloned.1.call-update) | async-done | bytes 262160 | tf_op jit(solution)/shard_map/psum | solution.py:107
  144.5 1.7 %multiply_add_fusion = f32[4,32,512]{2,1,0:T(8,128)} fusion(f32[4,32,512]{2,1,0:T(8,128)S(1)} %copy-done.5, f32[4,32,512]{2,1,0:T(8,128)S(1)} %all-to-all-done, f32[4,32,512]{2,1,0:T(8,128)} %all-reduce.2.cloned.1.call-done, f32[]{:T(128)S(6)} %sqrt.3, f32[]{:T(128)} %bitcast.6), kind=kLoop, calls=%fused_computation.34 | loop fusion | flops 262144 | bytes 1048584 | tf_op jit(solution)/shard_map/add | solution.py:108
  146.2 1.7 %copy.57 = f32[4,32,512]{2,1,0:T(8,128)} copy(f32[4,32,512]{2,1,0:T(8,128)} %all-reduce.2.cloned.1.call-done) | data formatting | bytes 524288
  (17 shorter events, 0.2 us)
Async XLA Ops:
  7.2 1.2 copy-start
  8.4 4.4 %copy-start.4 = (bf16[256,1024]{1,0:T(8,128)(2,1)S(1)}, bf16[256,1024]{1,0:T(8,128)(2,1)}, u32[]{:S(2)}) copy-start(bf16[256,1024]{1,0:T(8,128)(2,1)} %param.19) | copy-start | bytes 1572868
  12.8 3.3 %copy-start.2 = (f32[1,128,512]{2,1,0:T(8,128)S(1)}, f32[1,128,512]{2,1,0:T(8,128)}, u32[]{:S(2)}) copy-start(f32[1,128,512]{2,1,0:T(8,128)} %param.14) | copy-start | bytes 786436
  16.1 6.5 %copy-start.7 = (bf16[256,8]{0,1:T(8,128)(2,1)S(1)}, bf16[256,8]{0,1:T(8,128)(2,1)}, u32[]{:S(2)}) copy-start(bf16[256,8]{0,1:T(8,128)(2,1)} %param.21) | copy-start | bytes 12292
  16.1 6.6 %copy-start.1 = (bf16[512,1024]{1,0:T(8,128)(2,1)S(1)}, bf16[512,1024]{1,0:T(8,128)(2,1)}, u32[]{:S(2)}) copy-start(bf16[512,1024]{1,0:T(8,128)(2,1)} %param.18) | copy-start | bytes 3145732
  31.9 9.4 %collective-permute-start = (bf16[128,512]{1,0:T(8,128)(2,1)S(1)}, bf16[128,512]{1,0:T(8,128)(2,1)S(1)}, u32[]{:S(2)}, u32[]{:S(2)}) collective-permute-start(bf16[128,512]{1,0:T(8,128)(2,1)S(1)} %get-tuple-element.115), channel_id=1, source_target_pairs={{0,4},{4,8},{8,12},{12,0},{1,5},{5,9},{9,13},{13,1},{2,6},{6,10},{... | collective-permute-start | bytes 393224 | tf_op jit(solution)/shard_map/while/body/eval_jaxpr/ppermute | solution.py:15
  34.9 16.7 %collective-permute-start.1 = (f32[128,1024]{0,1:T(8,128)}, f32[128,1024]{0,1:T(8,128)S(1)}, u32[]{:S(2)}, u32[]{:S(2)}) collective-permute-start(f32[128,1024]{0,1:T(8,128)} %get-tuple-element.116), channel_id=1, source_target_pairs={{0,4},{4,8},{8,12},{12,0},{1,5},{5,9},{9,13},{13,1},{2,6},{6,10},{... | collective-permute-start | bytes 1572872 | tf_op jit(solution)/shard_map/while/body/eval_jaxpr/ppermute | solution.py:15
  52.5 8.2 %collective-permute-start = (bf16[128,512]{1,0:T(8,128)(2,1)S(1)}, bf16[128,512]{1,0:T(8,128)(2,1)S(1)}, u32[]{:S(2)}, u32[]{:S(2)}) collective-permute-start(bf16[128,512]{1,0:T(8,128)(2,1)S(1)} %get-tuple-element.115), channel_id=1, source_target_pairs={{0,4},{4,8},{8,12},{12,0},{1,5},{5,9},{9,13},{13,1},{2,6},{6,10},{... | collective-permute-start | bytes 393224 | tf_op jit(solution)/shard_map/while/body/eval_jaxpr/ppermute | solution.py:15
  52.5 17.7 %collective-permute-start.1 = (f32[128,1024]{0,1:T(8,128)}, f32[128,1024]{0,1:T(8,128)S(1)}, u32[]{:S(2)}, u32[]{:S(2)}) collective-permute-start(f32[128,1024]{0,1:T(8,128)} %get-tuple-element.116), channel_id=1, source_target_pairs={{0,4},{4,8},{8,12},{12,0},{1,5},{5,9},{9,13},{13,1},{2,6},{6,10},{... | collective-permute-start | bytes 1572872 | tf_op jit(solution)/shard_map/while/body/eval_jaxpr/ppermute | solution.py:15
  71.1 8.2 %collective-permute-start = (bf16[128,512]{1,0:T(8,128)(2,1)S(1)}, bf16[128,512]{1,0:T(8,128)(2,1)S(1)}, u32[]{:S(2)}, u32[]{:S(2)}) collective-permute-start(bf16[128,512]{1,0:T(8,128)(2,1)S(1)} %get-tuple-element.115), channel_id=1, source_target_pairs={{0,4},{4,8},{8,12},{12,0},{1,5},{5,9},{9,13},{13,1},{2,6},{6,10},{... | collective-permute-start | bytes 393224 | tf_op jit(solution)/shard_map/while/body/eval_jaxpr/ppermute | solution.py:15
  71.1 16.8 %collective-permute-start.1 = (f32[128,1024]{0,1:T(8,128)}, f32[128,1024]{0,1:T(8,128)S(1)}, u32[]{:S(2)}, u32[]{:S(2)}) collective-permute-start(f32[128,1024]{0,1:T(8,128)} %get-tuple-element.116), channel_id=1, source_target_pairs={{0,4},{4,8},{8,12},{12,0},{1,5},{5,9},{9,13},{13,1},{2,6},{6,10},{... | collective-permute-start | bytes 1572872 | tf_op jit(solution)/shard_map/while/body/eval_jaxpr/ppermute | solution.py:15
  88.8 21.9 %copy-start.6 = (bf16[1024,512]{1,0:T(8,128)(2,1)S(1)}, bf16[1024,512]{1,0:T(8,128)(2,1)}, u32[]{:S(2)}) copy-start(bf16[1024,512]{1,0:T(8,128)(2,1)} %param.25) | copy-start | bytes 3145732
  88.8 55.7 %copy-start.5 = (f32[4,32,512]{2,1,0:T(8,128)S(1)}, f32[4,32,512]{2,1,0:T(8,128)}, u32[]{:S(2)}) copy-start(f32[4,32,512]{2,1,0:T(8,128)} %param.17) | copy-start | bytes 786436
  100.5 10.2 %all-to-all-start = ((f32[4,32,512]{2,1,0:T(8,128)}), f32[4,32,512]{2,1,0:T(8,128)S(1)}, u32[]{:S(2)}, u32[]{:S(2)}) async-start(f32[4,32,512]{2,1,0:T(8,128)} %bitcast.120), calls=%async_computation | async-start | bytes 524288 | tf_op jit(solution)/shard_map/all_to_all | solution.py:69
  103.9 40.6 %all-reduce.2.cloned.1.call-start = ((), (), s32[]{:S(2)}) async-start(), calls=%async_computation.2 | async-start | bytes 524288 | tf_op jit(solution)/shard_map/psum | solution.py:107
  112.4 0.7 copy-start.3
Sparse Core Ops, SparseCore 0:
  113.2 31.2 all-reduce.1
where the time goes:
time: 155 us
  waiting for transfers between devices  65.3 us (42%)
  matrix products  41.7 us (27%)
  between operations  15.1 us (10%)
  blocking collectives  9.51 us (6%)
  starting transfers between devices  9.34 us (6%)
  local copies, waits for them, and re-layouts  9.31 us (6%)
  other arithmetic  4.42 us (3%)
    psum x1, waiting for transfers between devices, on_device(): lax.psum(scores_flat, ('hid', 'rep')).reshape(obs_count, stripe, width)  31.3 us
    ppermute x6, waiting for transfers between devices, passed_along(): lax.ppermute(shard, axis, [(i, (i + by) % size) for i in range(size)])  28.5 us
    dot_general x4, matrix products, pair_pool(): jnp.einsum('phj,jhd->phd', weights, value_heads, preferred_element_type=j...  27.6 us
    all_to_all x1, blocking collectives, on_device(): lax.all_to_all(pieces, 'obs', split_axis=0, concat_axis=0, tiled=True)  9.51 us
    while x1, local copies, waits for them, and re-layouts, on_device(): cycle_state = lax.fori_loop(0, obs_count - 1, turn, (moving, pool(moving)))  6.51 us
    ppermute x6, starting transfers between devices, passed_along(): lax.ppermute(shard, axis, [(i, (i + by) % size) for i in range(size)])  5.89 us
    all_to_all x1, waiting for transfers between devices, on_device(): lax.all_to_all(owned, 'obs', split_axis=0, concat_axis=0, tiled=True)  5.4 us
    dot_general x1, matrix products, on_device(): jnp.dot(obs_embed, w_value, preferred_element_type=jnp.float32)  4.35 us
  transfers between devices with their start and end apart: 8, of which 8 were waited for; matrix products, arithmetic and copies ran while one was open for 14% of the time, Pallas kernels for 0%

commit v1 on v0

--- a/solution.py
+++ b/solution.py
@@ -8,6 +8,22 @@
 STEPS = 64
 SIG_LO = 0.05
 SIG_HI = 1.0
+
+
+def swapped_with_each(x, axis, split, join):
+    ways, here = (lax.axis_size(axis), lax.axis_index(axis))
+    width = x.shape[split] // ways
+    shape = list(x.shape)
+    shape[split] = width
+    height = shape[join]
+    shape[join] = height * ways
+    full = jnp.zeros(shape, x.dtype)
+    for mask in range(ways):
+        part = lax.dynamic_slice_in_dim(x, (here ^ mask) * width, width, axis=split)
+        if mask:
+            part = lax.ppermute(part, axis, [(d, d ^ mask) for d in range(ways)])
+        full = lax.dynamic_update_slice_in_dim(full, part, (here ^ mask) * height, axis=join)
+    return full
 
 
 def passed_along(shard, axis, by):
@@ -87,7 +103,7 @@
         flat, score_weight, precision=lax.Precision.HIGHEST, preferred_element_type=jnp.float32
     )
     pieces = result.reshape(pieces.shape[:-1] + (width,))
-    received = lax.all_to_all(pieces, "obs", split_axis=0, concat_axis=0, tiled=True)
+    received = swapped_with_each(pieces, "obs", 0, 0)
     summed = jnp.roll(received, 1, axis=0)
     owner_rows = theta_owner.reshape(block_rows, width)
     share = block_rows // rep_count

time: 155 us -> 150 us (0.968)
  blocking collectives: 9.51 us -> 0 us
  starting transfers between devices: 9.34 us -> 13.8 us
    all_to_all x1 -> x0, blocking collectives: 9.51 us -> none  [on_device(): lax.all_to_all(pieces, 'obs', split_axis=0, concat_axis=0, tiled=True)]
    ppermute x0 -> x3, starting transfers between devices: none -> 4.44 us  [swapped_with_each(): part = lax.ppermute(part, axis, [(d, d ^ mask) for d in range(ways)])]
  transfers between devices with their start and end apart: 8 -> 11, of which waited for: 8 -> 8; matrix products, arithmetic and copies ran while one was open for 14% -> 14% of each run, Pallas kernels for 0% -> 0%
where the time goes in v1:
time: 150 us
  waiting for transfers between devices  65.2 us (43%)
  matrix products  41.8 us (28%)
  between operations  15.1 us (10%)
  starting transfers between devices  13.8 us (9%)
  local copies, waits for them, and re-layouts  9.39 us (6%)
  other arithmetic  4.46 us (3%)
    psum x1, waiting for transfers between devices, on_device(): lax.psum(scores_flat, ('hid', 'rep')).reshape(obs_count, stripe, width)  31.3 us
    ppermute x6, waiting for transfers between devices, passed_along(): lax.ppermute(shard, axis, [(i, (i + by) % size) for i in range(size)])  28.5 us
    dot_general x4, matrix products, pair_pool(): jnp.einsum('phj,jhd->phd', weights, value_heads, preferred_element_type=j...  27.7 us
    while x1, local copies, waits for them, and re-layouts, on_device(): cycle_state = lax.fori_loop(0, obs_count - 1, turn, (moving, pool(moving)))  6.53 us
    ppermute x6, starting transfers between devices, passed_along(): lax.ppermute(shard, axis, [(i, (i + by) % size) for i in range(size)])  5.9 us
    all_to_all x1, waiting for transfers between devices, on_device(): lax.all_to_all(owned, 'obs', split_axis=0, concat_axis=0, tiled=True)  5.32 us
    ppermute x3, starting transfers between devices, swapped_with_each(): part = lax.ppermute(part, axis, [(d, d ^ mask) for d in range(ways)])  4.44 us
    dot_general x1, matrix products, on_device(): jnp.dot(obs_embed, w_value, preferred_element_type=jnp.float32)  4.36 us
  transfers between devices with their start and end apart: 11, of which 8 were waited for; matrix products, arithmetic and copies ran while one was open for 14% of the time, Pallas kernels for 0%

profile of v1, /device:TPU:0, one launch (start us, length us, event | category | flops | bytes accessed | tf_op | source)
XLA Modules:
  0.0 149.8 jit_solution(14334431264857857293)
XLA Ops:
  7.2 0.0 copy-start
  8.1 0.3 copy-done
  8.4 4.4 %convolution_convert_fusion.2 = bf16[2048,1024]{0,1:T(8,128)(2,1)} fusion(bf16[2048,256]{1,0:T(8,128)(2,1)S(1)} %copy-done, bf16[256,1024]{1,0:T(8,128)(2,1)} %param.20), kind=kOutput, calls=%fused_computation.23 | convolution fusion | flops 1075838976 | bytes 5767168 | tf_op jit(solution)/shard_map/dot_general | solution.py:79
  12.8 3.3 %convolution_convert_fusion.1 = bf16[2048,1024]{0,1:T(8,128)(2,1)} fusion(bf16[2048,256]{1,0:T(8,128)(2,1)S(1)} %copy-done, bf16[256,1024]{1,0:T(8,128)(2,1)S(1)} %copy-done.4), kind=kOutput, calls=%fused_computation.22 | convolution fusion | flops 1075838976 | bytes 5767168 | tf_op jit(solution)/shard_map/dot_general | solution.py:78
  16.1 0.0 copy-start.7
  16.1 0.0 copy-start.1
  16.1 6.5 %copy.19 = bf16[2048,1024]{1,0:T(8,128)(2,1)} copy(bf16[2048,1024]{0,1:T(8,128)(2,1)} %convolution_convert_fusion.1) | data formatting | bytes 8388608 | tf_op jit(solution)/shard_map/while | solution.py:99
  22.6 0.1 fusion.35
  22.7 0.3 fusion.21
  23.1 8.8 %fusion.20 = f32[8,128,128]{2,1,0:T(8,128)} fusion(bf16[2048,8,128]{0,2,1:T(8,128)(2,1)} %bitcast.116, bf16[2048,8,128]{0,2,1:T(8,128)(2,1)} %bitcast.115, f32[8]{0:T(128)S(1)} %bitcast.124, bf16[16,8,8,128]{3,2,1,0:T(8,128)(2,1)S(1)} %fusion.21), kind=kOutput, calls=%fused_computation.24 | convolution fusion | flops 1088421888 | bytes 9175072 | tf_op jit(solution)/shard_map/phj,jhd->phd/dot_general | solution.py:56
  31.9 56.9 %while.12 = (s32[]{:T(128)}, bf16[128,512]{1,0:T(8,128)(2,1)S(1)}, f32[128,1024]{0,1:T(8,128)}, bf16[512,1024]{1,0:T(8,128)(2,1)S(1)}, bf16[2048,1024]{1,0:T(8,1...) while((s32[]{:T(128)}, bf16[128,512]{1,0:T(8,128)(2,1)S(1)}, ...), condition=%wide.region_1.2_spmd, body=%wide.region_0.1_spmd.sunk | while | flops 1222901760 | bytes 15073477 | solution.py:99
  31.9 3.0 %collective-permute-start = (bf16[128,512]{1,0:T(8,128)(2,1)S(1)}, bf16[128,512]{1,0:T(8,128)(2,1)S(1)}, u32[]{:S(2)}, u32[]{:S(2)}) collective-permute-start(bf16[128,512]{1,0:T(8,128)(2,1)S(1)} %get-tuple-element.119), channel_id=1, source_target_pairs={{0,4},{4,8},{8,12},{12,0},{1,5},{5,9},{9,13},{13,1},{2,6},{6,10},{... | collective-permute-start | bytes 393224 | tf_op jit(solution)/shard_map/while/body/eval_jaxpr/ppermute | solution.py:31
  34.9 1.6 %collective-permute-start.1 = (f32[128,1024]{0,1:T(8,128)}, f32[128,1024]{0,1:T(8,128)S(1)}, u32[]{:S(2)}, u32[]{:S(2)}) collective-permute-start(f32[128,1024]{0,1:T(8,128)} %get-tuple-element.120), channel_id=1, source_target_pairs={{0,4},{4,8},{8,12},{12,0},{1,5},{5,9},{9,13},{13,1},{2,6},{6,10},{... | collective-permute-start | bytes 1572872 | tf_op jit(solution)/shard_map/while/body/eval_jaxpr/ppermute | solution.py:31
  36.5 4.8 %collective-permute-done = bf16[128,512]{1,0:T(8,128)(2,1)S(1)} collective-permute-done((bf16[128,512]{1,0:T(8,128)(2,1)S(1)}, bf16[128,512]{1,0:T(8,128)(2,1)S(1)}, u32[]{:S(2)}, u32[]{:S(2)}) %collective-permute-start) | collective-permute-done | bytes 131104 | tf_op jit(solution)/shard_map/while/body/eval_jaxpr/ppermute | solution.py:31
  41.3 0.3 fusion.72
  41.6 6.3 %fusion.73 = f32[8,128,128]{1,2,0:T(8,128)S(1)} fusion(bf16[2048,8,128]{0,2,1:T(8,128)(2,1)} %bitcast.117, f32[8]{0:T(128)S(1)} %bitcast.125, bf16[16,8,8,128]{3,2,1,0:T(8,128)(2,1)S(1)} %fusion.72, bf16[2048,1024]{1,0:T(8,128)(2,1)} %get-tuple-element.130), kind=kOutput, calls=%fused_computation.8.clone.1 | convolution fusion | flops 1088421888 | bytes 9175072 | tf_op jit(solution)/shard_map/while/body/eval_jaxpr/phj,jhd->phd/dot_general | solution.py:56
  47.9 3.8 %collective-permute-done.1 = f32[128,1024]{0,1:T(8,128)S(1)} collective-permute-done((f32[128,1024]{0,1:T(8,128)}, f32[128,1024]{0,1:T(8,128)S(1)}, u32[]{:S(2)}, u32[]{:S(2)}) %collective-permute-start.1) | collective-permute-done | bytes 524320 | tf_op jit(solution)/shard_map/while/body/eval_jaxpr/ppermute | solution.py:31
  51.7 0.9 bitcast_add_fusion.2
  52.6 0.0 collective-permute-start
  52.6 1.3 collective-permute-start.1
  53.9 6.9 %collective-permute-done = bf16[128,512]{1,0:T(8,128)(2,1)S(1)} collective-permute-done((bf16[128,512]{1,0:T(8,128)(2,1)S(1)}, bf16[128,512]{1,0:T(8,128)(2,1)S(1)}, u32[]{:S(2)}, u32[]{:S(2)}) %collective-permute-start) | collective-permute-done | bytes 131104 | tf_op jit(solution)/shard_map/while/body/eval_jaxpr/ppermute | solution.py:31
  60.8 0.3 fusion.72
  61.1 6.3 %fusion.73 = f32[8,128,128]{1,2,0:T(8,128)S(1)} fusion(bf16[2048,8,128]{0,2,1:T(8,128)(2,1)} %bitcast.117, f32[8]{0:T(128)S(1)} %bitcast.125, bf16[16,8,8,128]{3,2,1,0:T(8,128)(2,1)S(1)} %fusion.72, bf16[2048,1024]{1,0:T(8,128)(2,1)} %get-tuple-element.130), kind=kOutput, calls=%fused_computation.8.clone.1 | convolution fusion | flops 1088421888 | bytes 9175072 | tf_op jit(solution)/shard_map/while/body/eval_jaxpr/phj,jhd->phd/dot_general | solution.py:56
  67.4 2.9 %collective-permute-done.1 = f32[128,1024]{0,1:T(8,128)S(1)} collective-permute-done((f32[128,1024]{0,1:T(8,128)}, f32[128,1024]{0,1:T(8,128)S(1)}, u32[]{:S(2)}, u32[]{:S(2)}) %collective-permute-start.1) | collective-permute-done | bytes 524320 | tf_op jit(solution)/shard_map/while/body/eval_jaxpr/ppermute | solution.py:31
  70.3 0.9 bitcast_add_fusion.2
  71.2 0.0 collective-permute-start
  71.2 0.0 collective-permute-start.1
  71.2 8.2 %collective-permute-done = bf16[128,512]{1,0:T(8,128)(2,1)S(1)} collective-permute-done((bf16[128,512]{1,0:T(8,128)(2,1)S(1)}, bf16[128,512]{1,0:T(8,128)(2,1)S(1)}, u32[]{:S(2)}, u32[]{:S(2)}) %collective-permute-start) | collective-permute-done | bytes 131104 | tf_op jit(solution)/shard_map/while/body/eval_jaxpr/ppermute | solution.py:31
  79.4 0.3 fusion.72
  79.7 6.3 %fusion.73 = f32[8,128,128]{1,2,0:T(8,128)S(1)} fusion(bf16[2048,8,128]{0,2,1:T(8,128)(2,1)} %bitcast.117, f32[8]{0:T(128)S(1)} %bitcast.125, bf16[16,8,8,128]{3,2,1,0:T(8,128)(2,1)S(1)} %fusion.72, bf16[2048,1024]{1,0:T(8,128)(2,1)} %get-tuple-element.130), kind=kOutput, calls=%fused_computation.8.clone.1 | convolution fusion | flops 1088421888 | bytes 9175072 | tf_op jit(solution)/shard_map/while/body/eval_jaxpr/phj,jhd->phd/dot_general | solution.py:56
  86.0 1.9 %collective-permute-done.1 = f32[128,1024]{0,1:T(8,128)S(1)} collective-permute-done((f32[128,1024]{0,1:T(8,128)}, f32[128,1024]{0,1:T(8,128)S(1)}, u32[]{:S(2)}, u32[]{:S(2)}) %collective-permute-start.1) | collective-permute-done | bytes 524320 | tf_op jit(solution)/shard_map/while/body/eval_jaxpr/ppermute | solution.py:31
  88.0 0.9 bitcast_add_fusion.2
  88.9 2.2 %fusion.36 = f32[128,512]{1,0:T(8,128)S(1)} fusion(f32[128,1024]{0,1:T(8,128)} %get-tuple-element.39, bf16[1024,512]{1,0:T(8,128)(2,1)} %param.22), kind=kOutput, calls=%fused_computation.56 | convolution fusion | flops 805306368 | bytes 1835008 | tf_op jit(solution)/shard_map/dot_general | solution.py:102
  91.1 0.1 collective-permute-start.2
  91.2 0.2 collective-permute-start.3
  91.4 4.2 %collective-permute-start.4 = (f32[1,32,512]{2,1,0:T(8,128)S(1)}, f32[1,32,512]{2,1,0:T(8,128)S(1)}, u32[]{:S(2)}, u32[]{:S(2)}) collective-permute-start(f32[1,32,512]{2,1,0:T(8,128)S(1)} %get-tuple-element.61), channel_id=1, source_target_pairs={{0,12},{4,8},{8,4},{12,0},{1,13},{5,9},{9,5},{13,1},{2,14},{6,10},... | collective-permute-start | bytes 196616 | tf_op jit(solution)/shard_map/ppermute | solution.py:24
  95.6 3.4 %all-to-all-start = ((f32[4,32,512]{2,1,0:T(8,128)}), f32[4,32,512]{2,1,0:T(8,128)S(1)}, u32[]{:S(2)}, u32[]{:S(2)}) async-start(f32[4,32,512]{2,1,0:T(8,128)} %bitcast.120), calls=%async_computation | async-start | bytes 524288 | tf_op jit(solution)/shard_map/all_to_all | solution.py:85
  99.0 0.0 all-reduce.2.cloned.1.call-start
  99.0 1.2 fusion.37
  100.2 0.0 collective-permute-done.2
  100.4 5.3 %all-to-all-done = f32[4,32,512]{2,1,0:T(8,128)S(1)} async-done(((f32[4,32,512]{2,1,0:T(8,128)}), f32[4,32,512]{2,1,0:T(8,128)S(1)}, u32[]{:S(2)}, u32[]{:S(2)}) %all-to-all-start) | async-done | bytes 262176 | tf_op jit(solution)/shard_map/all_to_all | solution.py:85
  105.7 1.7 %fusion.23 = f32[128,512]{1,0:T(8,128)S(1)} fusion(f32[128,512]{1,0:T(8,128)S(1)} %bitcast.121, s32[]{:T(128)S(6)} %select_n.25, bf16[1024,512]{1,0:T(8,128)(2,1)S(1)} %copy-done.6, bf16[512,1024]{1,0:T(8,128)(2,1)} %param.23, f32[1024]{0:T(1024)S(1)} %bitcast.123, f32[128,512]{1,0:T(8,128)S(1)} %bitcast.118), kind=kOutput, calls=%fused_computation.30 | convolution fusion | flops 134676480 | bytes 2429952 | tf_op jit(solution)/shard_map/dot_general | solution.py:116
  107.4 0.0 copy-start.3
  107.5 0.7 copy-done.3
  108.2 0.0 all-reduce.2.cloned.1.call-update
  108.3 31.3 %all-reduce.2.cloned.1.call-done = f32[4,32,512]{2,1,0:T(8,128)} async-done(((f32[4,32,512]{2,1,0:T(8,128)}), f32[4,32,512]{2,1,0:T(8,128)}) %all-reduce.2.cloned.1.call-update) | async-done | bytes 262160 | tf_op jit(solution)/shard_map/psum | solution.py:123
  139.6 1.7 %multiply_add_fusion = f32[4,32,512]{2,1,0:T(8,128)} fusion(f32[4,32,512]{2,1,0:T(8,128)S(1)} %copy-done.5, f32[4,32,512]{2,1,0:T(8,128)S(1)} %all-to-all-done, f32[4,32,512]{2,1,0:T(8,128)} %all-reduce.2.cloned.1.call-done, f32[]{:T(128)S(6)} %sqrt.3, f32[]{:T(128)} %bitcast.6), kind=kLoop, calls=%fused_computation.34 | loop fusion | flops 262144 | bytes 1048584 | tf_op jit(solution)/shard_map/add | solution.py:124
  141.3 1.7 %copy.61 = f32[4,32,512]{2,1,0:T(8,128)} copy(f32[4,32,512]{2,1,0:T(8,128)} %all-reduce.2.cloned.1.call-done) | data formatting | bytes 524288
  (27 shorter events, 0.3 us)
Async XLA Ops:
  7.2 1.2 copy-start
  8.4 4.4 %copy-start.4 = (bf16[256,1024]{1,0:T(8,128)(2,1)S(1)}, bf16[256,1024]{1,0:T(8,128)(2,1)}, u32[]{:S(2)}) copy-start(bf16[256,1024]{1,0:T(8,128)(2,1)} %param.19) | copy-start | bytes 1572868
  12.8 3.3 %copy-start.2 = (f32[1,128,512]{2,1,0:T(8,128)S(1)}, f32[1,128,512]{2,1,0:T(8,128)}, u32[]{:S(2)}) copy-start(f32[1,128,512]{2,1,0:T(8,128)} %param.14) | copy-start | bytes 786436
  16.1 6.6 %copy-start.7 = (bf16[256,8]{0,1:T(8,128)(2,1)S(1)}, bf16[256,8]{0,1:T(8,128)(2,1)}, u32[]{:S(2)}) copy-start(bf16[256,8]{0,1:T(8,128)(2,1)} %param.21) | copy-start | bytes 12292
  16.1 6.7 %copy-start.1 = (bf16[512,1024]{1,0:T(8,128)(2,1)S(1)}, bf16[512,1024]{1,0:T(8,128)(2,1)}, u32[]{:S(2)}) copy-start(bf16[512,1024]{1,0:T(8,128)(2,1)} %param.18) | copy-start | bytes 3145732
  31.9 9.4 %collective-permute-start = (bf16[128,512]{1,0:T(8,128)(2,1)S(1)}, bf16[128,512]{1,0:T(8,128)(2,1)S(1)}, u32[]{:S(2)}, u32[]{:S(2)}) collective-permute-start(bf16[128,512]{1,0:T(8,128)(2,1)S(1)} %get-tuple-element.119), channel_id=1, source_target_pairs={{0,4},{4,8},{8,12},{12,0},{1,5},{5,9},{9,13},{13,1},{2,6},{6,10},{... | collective-permute-start | bytes 393224 | tf_op jit(solution)/shard_map/while/body/eval_jaxpr/ppermute | solution.py:31
  34.9 16.8 %collective-permute-start.1 = (f32[128,1024]{0,1:T(8,128)}, f32[128,1024]{0,1:T(8,128)S(1)}, u32[]{:S(2)}, u32[]{:S(2)}) collective-permute-start(f32[128,1024]{0,1:T(8,128)} %get-tuple-element.120), channel_id=1, source_target_pairs={{0,4},{4,8},{8,12},{12,0},{1,5},{5,9},{9,13},{13,1},{2,6},{6,10},{... | collective-permute-start | bytes 1572872 | tf_op jit(solution)/shard_map/while/body/eval_jaxpr/ppermute | solution.py:31
  52.6 8.2 %collective-permute-start = (bf16[128,512]{1,0:T(8,128)(2,1)S(1)}, bf16[128,512]{1,0:T(8,128)(2,1)S(1)}, u32[]{:S(2)}, u32[]{:S(2)}) collective-permute-start(bf16[128,512]{1,0:T(8,128)(2,1)S(1)} %get-tuple-element.119), channel_id=1, source_target_pairs={{0,4},{4,8},{8,12},{12,0},{1,5},{5,9},{9,13},{13,1},{2,6},{6,10},{... | collective-permute-start | bytes 393224 | tf_op jit(solution)/shard_map/while/body/eval_jaxpr/ppermute | solution.py:31
  52.6 17.7 %collective-permute-start.1 = (f32[128,1024]{0,1:T(8,128)}, f32[128,1024]{0,1:T(8,128)S(1)}, u32[]{:S(2)}, u32[]{:S(2)}) collective-permute-start(f32[128,1024]{0,1:T(8,128)} %get-tuple-element.120), channel_id=1, source_target_pairs={{0,4},{4,8},{8,12},{12,0},{1,5},{5,9},{9,13},{13,1},{2,6},{6,10},{... | collective-permute-start | bytes 1572872 | tf_op jit(solution)/shard_map/while/body/eval_jaxpr/ppermute | solution.py:31
  71.2 8.2 %collective-permute-start = (bf16[128,512]{1,0:T(8,128)(2,1)S(1)}, bf16[128,512]{1,0:T(8,128)(2,1)S(1)}, u32[]{:S(2)}, u32[]{:S(2)}) collective-permute-start(bf16[128,512]{1,0:T(8,128)(2,1)S(1)} %get-tuple-element.119), channel_id=1, source_target_pairs={{0,4},{4,8},{8,12},{12,0},{1,5},{5,9},{9,13},{13,1},{2,6},{6,10},{... | collective-permute-start | bytes 393224 | tf_op jit(solution)/shard_map/while/body/eval_jaxpr/ppermute | solution.py:31
  71.2 16.8 %collective-permute-start.1 = (f32[128,1024]{0,1:T(8,128)}, f32[128,1024]{0,1:T(8,128)S(1)}, u32[]{:S(2)}, u32[]{:S(2)}) collective-permute-start(f32[128,1024]{0,1:T(8,128)} %get-tuple-element.120), channel_id=1, source_target_pairs={{0,4},{4,8},{8,12},{12,0},{1,5},{5,9},{9,13},{13,1},{2,6},{6,10},{... | collective-permute-start | bytes 1572872 | tf_op jit(solution)/shard_map/while/body/eval_jaxpr/ppermute | solution.py:31
  88.9 16.9 %copy-start.6 = (bf16[1024,512]{1,0:T(8,128)(2,1)S(1)}, bf16[1024,512]{1,0:T(8,128)(2,1)}, u32[]{:S(2)}) copy-start(bf16[1024,512]{1,0:T(8,128)(2,1)} %param.25) | copy-start | bytes 3145732
  88.9 50.8 %copy-start.5 = (f32[4,32,512]{2,1,0:T(8,128)S(1)}, f32[4,32,512]{2,1,0:T(8,128)}, u32[]{:S(2)}) copy-start(f32[4,32,512]{2,1,0:T(8,128)} %param.17) | copy-start | bytes 786436
  91.1 9.1 %collective-permute-start.2 = (f32[1,32,512]{2,1,0:T(8,128)S(1)}, f32[1,32,512]{2,1,0:T(8,128)S(1)}, u32[]{:S(2)}, u32[]{:S(2)}) collective-permute-start(f32[1,32,512]{2,1,0:T(8,128)S(1)} %get-tuple-element.63), channel_id=1, source_target_pairs={{0,4},{4,0},{8,12},{12,8},{1,5},{5,1},{9,13},{13,9},{2,6},{6,2},{1... | collective-permute-start | bytes 196616 | tf_op jit(solution)/shard_map/ppermute | solution.py:24
  91.2 9.1 %collective-permute-start.3 = (f32[1,32,512]{2,1,0:T(8,128)S(1)}, f32[1,32,512]{2,1,0:T(8,128)S(1)}, u32[]{:S(2)}, u32[]{:S(2)}) collective-permute-start(f32[1,32,512]{2,1,0:T(8,128)S(1)} %get-tuple-element.62), channel_id=1, source_target_pairs={{0,8},{4,12},{8,0},{12,4},{1,9},{5,13},{9,1},{13,5},{2,10},{6,14},... | collective-permute-start | bytes 196616 | tf_op jit(solution)/shard_map/ppermute | solution.py:24
  91.4 8.9 %collective-permute-start.4 = (f32[1,32,512]{2,1,0:T(8,128)S(1)}, f32[1,32,512]{2,1,0:T(8,128)S(1)}, u32[]{:S(2)}, u32[]{:S(2)}) collective-permute-start(f32[1,32,512]{2,1,0:T(8,128)S(1)} %get-tuple-element.61), channel_id=1, source_target_pairs={{0,12},{4,8},{8,4},{12,0},{1,13},{5,9},{9,5},{13,1},{2,14},{6,10},... | collective-permute-start | bytes 196616 | tf_op jit(solution)/shard_map/ppermute | solution.py:24
  95.6 10.2 %all-to-all-start = ((f32[4,32,512]{2,1,0:T(8,128)}), f32[4,32,512]{2,1,0:T(8,128)S(1)}, u32[]{:S(2)}, u32[]{:S(2)}) async-start(f32[4,32,512]{2,1,0:T(8,128)} %bitcast.120), calls=%async_computation | async-start | bytes 524288 | tf_op jit(solution)/shard_map/all_to_all | solution.py:85
  99.0 40.6 %all-reduce.2.cloned.1.call-start = ((), (), s32[]{:S(2)}) async-start(), calls=%async_computation.1 | async-start | bytes 524288 | tf_op jit(solution)/shard_map/psum | solution.py:123
  107.4 0.7 copy-start.3
Sparse Core Ops, SparseCore 0:
  108.3 31.2 all-reduce.1
